TPU v7x, 512 devices: a whole 4x8x8 slice. The times are simulated.
512 devices in a mesh: seq: 8 (over z_hi, core), head: 16 (over z_lo, y), dp: 4 (over x).
Axes of the slice: x: 4, y: 8, z: 8 (z_hi: 4, z_lo: 2; z = z_hi * 2 + z_lo), core: 2. Of those that a mesh axis runs over, the one named last changes fastest.
Arguments:
- tokens: bfloat16 [4, 1024, 4096], P('dp', 'seq', 'head'), may hold values from -6 to 6
- w_qkv: bfloat16 [4096, 3, 2048], P(('seq', 'dp'), None, 'head'), may hold values from -0.09375 to 0.09375
- w_lr: bfloat16 [4096, 16], P(None, 'head'), may hold values from -0.1875 to 0.1875
- w_out: bfloat16 [4096, 2048], P(('seq', 'dp'), 'head'), may hold values from -0.125 to 0.125
- w1_init: float32 [16, 128, 512], P('head'), may hold values from -0.5 to 0.5
- w2_init: float32 [16, 512, 128], P('head'), may hold values from -0.25 to 0.25
- d_out: bfloat16 [4, 1024, 4096], P('dp', 'seq', 'head'), may hold values from -6 to 6
Outputs:
- out: bfloat16 [4, 1024, 4096], P('dp', 'seq', 'head')
- d_tokens: bfloat16 [4, 1024, 4096], P('dp', 'seq', 'head')
- d_w1_init: float32 [16, 128, 512], P('head', None, ('seq', 'dp'))
- d_w2_init: float32 [16, 512, 128], P('head', ('seq', 'dp'))
All inputs are finite; a program needn't handle non-finite values.
Results may differ from a plain program's by a relative error of at most 0.018.
Values may be sent and summed in bfloat16 or wider, within the bound.
A program may use at most 64 MiB of HBM per device.

v0:
```python
import jax
import jax.numpy as jnp
from jax import lax
from jax.experimental import pallas as pl
from jax.experimental.pallas import tpu as pltpu
from jax.sharding import PartitionSpec as P

MB = 64
HD = 128
BF16 = jnp.bfloat16
F32 = jnp.float32
MESH = pl.DeviceIdType.MESH
EPSILON = 1e-06
BASE_RATE = 0.1
GELU_SCALE = 0.7978845608028654
GELU_CUBIC = 0.044715
CONTRACT_LAST = (((1,), (1,)), ((), ()))
CONTRACT_FIRST = (((0,), (0,)), ((), ()))


def matmul(left, right):
    return jnp.dot(left.astype(BF16), right.astype(BF16), preferred_element_type=F32)


def matmul_last(left, right):
    return lax.dot_general(left.astype(BF16), right.astype(BF16), CONTRACT_LAST, preferred_element_type=F32)


def matmul_first(left, right):
    return lax.dot_general(left.astype(BF16), right.astype(BF16), CONTRACT_FIRST, preferred_element_type=F32)


def row_mean(rows):
    return jnp.mean(rows, axis=-1, keepdims=True)


def row_sum(rows):
    return jnp.sum(rows, axis=-1, keepdims=True)


def spread(rates):
    return jnp.concatenate([rates] * 4, axis=1)


def gelu_parts(v, order):
    square = v * v
    bend = jnp.tanh(GELU_SCALE * (v + GELU_CUBIC * square * v))
    tilt = GELU_SCALE * (1.0 + 3.0 * GELU_CUBIC * square)
    flat = 1.0 - bend * bend
    half = 0.5 * v
    value = half * (1.0 + bend)
    slope = 0.5 * (1.0 + bend) + half * flat * tilt
    if order == 1:
        return value, slope
    curve = flat * (tilt + half * (6.0 * GELU_SCALE * GELU_CUBIC) * v - v * bend * tilt * tilt)
    return value, slope, curve


def norm_rows(rows):
    centred = rows - row_mean(rows)
    inv_scale = lax.rsqrt(row_mean(centred * centred) + EPSILON)
    return centred * inv_scale, inv_scale


def layer_kernel(
    tok_ref, wqkv_ref, wlr_ref, wout_ref, w1_ref, w2_ref, dout_ref,
    out_ref, dtok_ref, share1_ref, share2_ref,
    feat, cot, wq, wo, ttt_ref, dproj_ref, dlogit_ref, dw1_ref, dw2_ref,
    send_out, recv_out, pair_send, pair_recv, send_tok, recv_tok, dw_send, dw_recv, dw_sum, share,
    ckt, cqo, s1, s2, w1b, w2b,
    sv_slope, sv_curve, sv_m, sv_x2, sv_narrow,
    qp_xq, qp_dy, qp_wide, qp_g2, qp_dz, qp_ds, qp_kept,
    near_send, feat_recv, cot_recv, wq_recv, wq_recv_low, wo_recv, wo_recv_low,
    chunk_send, chunk_recv, qo_send, qo_recv,
    out_send, out_recv, pair_sends, pair_recvs, tok_send, tok_recv, dw_sems, dw_recvs, share_send, share_recv,
):
    place, head, group = (lax.axis_index(name) for name in ("seq", "head", "dp"))
    count, heads, groups = (lax.axis_size(name) for name in ("seq", "head", "dp"))
    rows = tok_ref.shape[0]
    half = rows // 2
    blocks = count * groups
    barrier = pltpu.get_barrier_semaphore()

    def greet_along(name, mine, size):
        def greet(step, carry):
            peer = lax.rem(mine + step, size)
            pl.semaphore_signal(barrier, inc=1, device_id={name: peer}, device_id_type=MESH)
            return carry

        lax.fori_loop(1, size, greet, 0)

    greet_along("seq", place, count)
    greet_along("head", head, heads)
    greet_along("dp", group, groups)
    pl.semaphore_wait(barrier, count + heads + groups - 3)

    started = []

    def push(src, dst, arrival, device):
        copy = pltpu.make_async_remote_copy(
            src_ref=src,
            dst_ref=dst,
            send_sem=near_send.at[len(started)],
            recv_sem=arrival,
            device_id=device,
            device_id_type=MESH,
        )
        copy.start()
        started.append(tuple(src.shape))

    def arrived(dst, arrival):
        pltpu.make_async_remote_copy(
            src_ref=dst,
            dst_ref=dst,
            send_sem=near_send.at[0],
            recv_sem=arrival,
            device_id={"seq": place},
            device_id_type=MESH,
        ).wait_recv()

    ring = heads // 2
    ring_at, ring_base = lax.rem(head, ring), lax.div(head, ring) * ring
    other_base = ring - ring_base
    partner = {"head": other_base + ring_at}
    ring_up = {"head": ring_base + lax.rem(ring_at + 1, ring)}
    ring_down = {"head": ring_base + lax.rem(ring_at + ring - 1, ring)}

    def ring_push(buffer, arrivals, block, device, src=None):
        push(buffer.at[block] if src is None else src, buffer.at[block], arrivals.at[block], device)

    def ring_start(buffer, arrivals, src):
        ring_push(buffer, arrivals, head, ring_up, src)
        ring_push(buffer, arrivals, head, ring_down, src)
        ring_push(buffer, arrivals, head, partner, src)

    def ring_partner(buffer, arrivals):
        block = other_base + ring_at
        arrived(buffer.at[block], arrivals.at[block])
        ring_push(buffer, arrivals, block, ring_up)
        ring_push(buffer, arrivals, block, ring_down)

    def ring_step(buffer, arrivals, base, step):
        below = base + lax.rem(ring_at + ring - step, ring)
        arrived(buffer.at[below], arrivals.at[below])
        if step < ring // 2:
            ring_push(buffer, arrivals, below, ring_up)
            above = base + lax.rem(ring_at + step, ring)
            arrived(buffer.at[above], arrivals.at[above])
            if step < ring // 2 - 1:
                ring_push(buffer, arrivals, above, ring_down)

    def feat_step(base, step):
        ring_step(feat, feat_recv, base, step)

    def cot_step(base, step):
        ring_step(cot, cot_recv, base, step)

    sib = place + 1 - 2 * lax.rem(place, 2)
    sibling = {"seq": sib}
    deep = [lax.rem(place + 2 * step, count) for step in range(4)]
    sib_deep = [lax.rem(sib + 2 * step, count) for step in range(4)]
    wide = [lax.rem(group + step, groups) for step in range(4)]
    deep_up, deep_down = {"seq": deep[1]}, {"seq": deep[3]}
    wide_up, wide_down = {"dp": wide[1]}, {"dp": wide[3]}

    def wq_push(block, device, src=None):
        push(wq.at[block] if src is None else src, wq.at[block], wq_recv.at[block], device)

    def wq_relay(from_below, from_above, up, down):
        push(wq.at[from_below, :half], wq.at[from_below, :half], wq_recv.at[from_below], up)
        push(wq.at[from_above, half:], wq.at[from_above, half:], wq_recv_low.at[from_above], down)

    def wq_arrived(block):
        arrived(wq.at[block], wq_recv.at[block])

    def wq_halves_arrived(block):
        arrived(wq.at[block, :half], wq_recv.at[block])
        arrived(wq.at[block, half:], wq_recv_low.at[block])

    def wq_spread(row, src=None):
        block = row * groups + group
        wq_push(block, wide_up, src)
        wq_push(block, wide_down, src)
        wq_push(block, sibling, src)

    def wq_sides(row):
        below, above = row * groups + wide[3], row * groups + wide[1]
        wq_arrived(below)
        wq_arrived(above)
        wq_relay(below, above, wide_up, wide_down)
        wq_push(below, sibling)
        wq_push(above, sibling)

    def wq_far(row):
        block = row * groups + wide[2]
        wq_halves_arrived(block)
        wq_push(block, sibling)

    layers = count // 2

    def halved(number):
        if isinstance(number, int):
            return number // 2, number % 2
        return lax.div(number, 2), lax.rem(number, 2)

    def wo_block(row, column):
        layer, side = halved(row)
        return (side * groups + column) * layers + layer

    def wo_column(row, column):
        return pl.ds((lax.rem(row, 2) * groups + column) * layers, layers)

    def wo_relay(from_below, from_above, up, down):
        push(wo.at[from_below, :half], wo.at[from_below, :half], wo_recv.at[from_below], up)
        push(wo.at[from_above, half:], wo.at[from_above, half:], wo_recv_low.at[from_above], down)

    def wo_column_push(column, device):
        at = wo_column(place, column)
        push(wo.at[at], wo.at[at], wo_recv.at[blocks + lax.rem(place, 2) * groups + column], device)

    def wo_column_arrived(row, column):
        at = wo_column(row, column)
        arrived(wo.at[at], wo_recv.at[blocks + lax.rem(row, 2) * groups + column])

    def wo_sides():
        wo_column_arrived(place, wide[3])
        wo_column_arrived(place, wide[1])
        pair = layers // 2
        low = (lax.rem(place, 2) * groups + wide[3]) * layers
        high = (lax.rem(place, 2) * groups + wide[1]) * layers + pair
        flag = blocks + lax.rem(place, 2) * groups
        push(wo.at[pl.ds(low, pair)], wo.at[pl.ds(low, pair)], wo_recv.at[flag + wide[3]], wide_up)
        push(wo.at[pl.ds(high, pair)], wo.at[pl.ds(high, pair)], wo_recv_low.at[flag + wide[1]], wide_down)
        wo_column_push(wide[3], sibling)
        wo_column_push(wide[1], sibling)

    def wo_far():
        pair = layers // 2
        low = (lax.rem(place, 2) * groups + wide[2]) * layers
        flag = blocks + lax.rem(place, 2) * groups
        arrived(wo.at[pl.ds(low, pair)], wo_recv.at[flag + wide[2]])
        arrived(wo.at[pl.ds(low + pair, pair)], wo_recv_low.at[flag + wide[2]])
        wo_column_push(wide[2], sibling)

    own = place * groups + group
    own_wo = wo_block(place, group)
    ring_start(feat, feat_recv, tok_ref)
    for part in range(3):
        wq[own, :, part * HD : (part + 1) * HD] = wqkv_ref[:, part, :]
    wq_push(own, deep_up)
    wq_push(own, deep_down)
    wq_spread(place)
    push(wout_ref, wo.at[own_wo], wo_recv.at[own_wo], deep_up)
    push(wout_ref, wo.at[own_wo], wo_recv.at[own_wo], deep_down)
    feat[head] = tok_ref[...]
    cot[head] = dout_ref[...]
    wo[own_wo] = wout_ref[...]
    feat_step(ring_base, 1)
    wq_sides(place)
    ring_partner(feat, feat_recv)
    feat_step(ring_base, 2)
    for row in (deep[3], deep[1]):
        wq_arrived(row * groups + group)
    wq_relay(deep[3] * groups + group, deep[1] * groups + group, deep_up, deep_down)
    wq_spread(deep[3])
    wq_spread(deep[1])
    wq_far(place)
    feat_step(other_base, 1)
    feat_step(ring_base, 3)
    for row in (deep[3], deep[1]):
        arrived(wo.at[wo_block(row, group)], wo_recv.at[wo_block(row, group)])
    wo_relay(wo_block(deep[3], group), wo_block(deep[1], group), deep_up, deep_down)
    feat_step(other_base, 2)
    wq_halves_arrived(deep[2] * groups + group)
    wq_spread(deep[2])
    wq_sides(deep[3])
    wq_sides(deep[1])
    feat_step(ring_base, 4)
    feat_step(other_base, 3)
    ring_start(cot, cot_recv, dout_ref)
    far = wo_block(deep[2], group)
    arrived(wo.at[far, :half], wo_recv.at[far])
    arrived(wo.at[far, half:], wo_recv_low.at[far])
    wq_sides(deep[2])
    wo_column_push(group, wide_up)
    wo_column_push(group, wide_down)
    wo_column_push(group, sibling)
    feat_step(other_base, 4)
    wq_far(deep[3])
    wq_far(deep[1])
    cot_step(ring_base, 1)
    wq_far(deep[2])
    for row in sib_deep:
        for column in (0, 1, 3, 2):
            wq_arrived(row * groups + wide[column])

    def depth_rows(buffer, piece):
        both = buffer[pl.ds(2 * piece, 2)]
        return both.reshape(2 * rows, both.shape[-1])

    def out_rows(piece):
        row, column = halved(piece)
        at = wo_block(row, 2 * column)
        return jnp.concatenate([wo[at], wo[at + layers]], axis=0)

    def rate_weights(piece):
        return jnp.concatenate([wlr_ref[pl.ds(2 * piece, 1), :], wlr_ref[pl.ds(2 * piece + 1, 1), :]], axis=1)

    def project(piece, carry):
        total, logit = carry
        part = feat[piece]
        total = total + jnp.dot(part, depth_rows(wq, piece), preferred_element_type=F32)
        weights = jnp.broadcast_to(rate_weights(piece), (HD, 2 * rows)).astype(BF16)
        return total, logit + matmul_last(part, weights)

    projected, logit = lax.fori_loop(
        0, heads, project, (jnp.zeros((rows, 3 * HD), F32), jnp.zeros((rows, HD), F32)), unroll=4
    )
    keys = projected[:, HD : 2 * HD]
    rates = (BASE_RATE / HD) * jax.nn.sigmoid(logit)
    rate_rows = jnp.transpose(rates)[:16, :]
    rate_high = rate_rows.astype(BF16)
    block_rows = ckt.at[place]
    block_rows[:rows, :HD] = keys.astype(BF16)
    block_rows[:rows, HD:] = (projected[:, 2 * HD :] - keys).astype(BF16)
    block_rows[rows:, :HD] = rate_high
    block_rows[rows:, HD:] = (rate_rows - rate_high.astype(F32)).astype(BF16)
    cqo[place, :, :HD] = projected[:, :HD].astype(BF16)

    def chunk_copy(source, to, which):
        return pltpu.make_async_remote_copy(
            src_ref=ckt.at[source],
            dst_ref=ckt.at[source],
            send_sem=chunk_send.at[which],
            recv_sem=chunk_recv.at[source],
            device_id={"seq": to},
            device_id_type=MESH,
        )

    s1[...] = w1_ref[...]
    s2[...] = w2_ref[...]
    chunk_copy(place, deep[1], count).start()
    chunk_copy(place, deep[3], count + 1).start()
    chunk_copy(place, sib, count + 2).start()
    chunk_copy(place, deep[2], count + 3).start()

    def same_side(source):
        return jnp.logical_and(source != place, lax.rem(source + place, 2) == 0)

    def take_chunk(source):
        @pl.when(source != place)
        def _():
            chunk_copy(source, place, 0).wait_recv()

        @pl.when(same_side(source))
        def _():
            chunk_copy(source, sib, source).start()

    place_row = lax.broadcasted_iota(jnp.int32, (MB, MB), 0)
    place_col = lax.broadcasted_iota(jnp.int32, (MB, MB), 1)

    def span_of(half_at):
        return slice(half_at * MB, (half_at + 1) * MB)

    def state_block(turn, half_at, e):
        block = 2 * turn + half_at
        k = ckt[turn, span_of(half_at), :HD]
        t = ckt[turn, span_of(half_at), HD:].astype(F32)
        first, second = s1[...].astype(BF16), s2[...].astype(BF16)
        x2, slope, curve = gelu_parts(matmul(k, first), 2)
        n, s = norm_rows(matmul(x2, second))
        r = n - t
        cross = row_mean(r * n)
        h = r - row_mean(r) - n * cross
        g2 = s * h
        m = matmul_last(g2, second)
        kt = jnp.transpose(k)
        x2t = jnp.transpose(x2)
        s1[...] = s1[...] - matmul(kt, spread(e) * (m * slope))
        s2[...] = s2[...] - matmul(x2t, e * g2)
        w1b[block] = first
        w2b[block] = second
        sv_slope[block] = slope
        sv_curve[block] = curve
        sv_m[block] = m
        sv_x2[block] = x2.astype(BF16)
        sv_narrow[block, 0] = n
        sv_narrow[block, 1] = r
        sv_narrow[block, 2] = h
        sv_narrow[block, 3] = g2
        sv_narrow[block, 4] = jnp.broadcast_to(s, (MB, HD))
        sv_narrow[block, 5] = jnp.broadcast_to(cross, (MB, HD))
        sv_narrow[block, 6] = e

    def query_forward(turn, half_at):
        block = 2 * turn + half_at
        span = span_of(half_at)
        q, k = cqo[turn, span, :HD], ckt[turn, span, :HD]
        first, second, x2 = w1b[block], w2b[block], sv_x2[block]
        g1 = (sv_m[block] * sv_slope[block]).astype(BF16)
        g2 = sv_narrow[block, 3].astype(BF16)
        e_row = jnp.transpose(sv_narrow[block, 6])[:MB, :]
        causal = jnp.where(place_col <= place_row, e_row, 0.0)
        raw1 = matmul_last(q, k)
        a1 = raw1 * causal
        xq, slope_q = gelu_parts(matmul(q, first) - matmul(a1, g1), 1)
        raw2 = matmul_last(xq, x2)
        a2 = raw2 * causal
        nq, sq = norm_rows(matmul(xq, second) - matmul(a2, g2))
        return q, first, second, x2, g1, g2, causal, raw1, a1, xq, slope_q, raw2, a2, nq, sq

    def query_part(turn, half_at):
        q, first, second, x2, g1, g2, causal, raw1, a1, xq, slope_q, raw2, a2, nq, sq = query_forward(
            turn, half_at
        )
        do = cqo[turn, span_of(half_at), HD:].astype(F32)
        dyq = (sq * (do - row_mean(do) - nq * row_mean(do * nq))).astype(BF16)
        da2 = -matmul_last(dyq, g2)
        ds2 = (da2 * causal).astype(BF16)
        dzq = ((matmul_last(dyq, second) + matmul(ds2, x2)) * slope_q).astype(BF16)
        da1 = -matmul_last(dzq, g1)
        qp_xq[half_at] = xq.astype(BF16)
        qp_dy[half_at] = dyq
        qp_wide[half_at, 0] = -matmul_first(a1, dzq)
        qp_wide[half_at, 1] = matmul_first(ds2, xq)
        qp_g2[half_at] = -matmul_first(a2, dyq)
        qp_dz[half_at] = dzq
        qp_ds[half_at] = (da1 * causal).astype(BF16)
        qp_kept[half_at] = jnp.where(place_col <= place_row, da2 * raw2 + da1 * raw1, 0.0)

    def chain_block(turn, half_at, mine):
        block = 2 * turn + half_at
        span = span_of(half_at)
        d1, d2 = dw1_ref[...], dw2_ref[...]
        d1b, d2b = d1.astype(BF16), d2.astype(BF16)
        k = ckt[turn, span, :HD]
        first, second, x2 = w1b[block], w2b[block], sv_x2[block]
        slope, curve, m = sv_slope[block], sv_curve[block], sv_m[block]
        n, r, h, g2, s, cross, e = (sv_narrow[block, i] for i in range(7))
        p1 = matmul(k, d1b)
        p2 = matmul_last(x2, d2b)
        dg1 = qp_wide[half_at, 0] - spread(e) * p1
        dmb = (dg1 * slope).astype(BF16)
        dg2 = qp_g2[half_at] - e * p2 + matmul(dmb, second)
        dh = s * dg2
        mean_n = row_mean(dh * n)
        dr = dh - row_mean(dh) - n * mean_n
        dn = dr - cross * dh - r * mean_n
        dy = s * (dn - row_mean(dn) - n * row_mean(dn * n)) - n * (row_mean(dg2 * h) * s * s)
        dyb = dy.astype(BF16)
        dx2 = qp_wide[half_at, 1] - matmul(e * g2, d2b) + matmul_last(dyb, second)
        dz1 = dx2 * slope + dg1 * m * curve
        dz1b = dz1.astype(BF16)
        narrow = jnp.concatenate([g2.astype(BF16), dyb, qp_dy[half_at]], axis=0)
        dw2_ref[...] = d2 + matmul_first(narrow, jnp.concatenate([dmb, x2, qp_xq[half_at]], axis=0))
        inputs = jnp.concatenate([k, cqo[turn, span, :HD]], axis=0)
        dw1_ref[...] = d1 + matmul_first(inputs, jnp.concatenate([dz1b, qp_dz[half_at]], axis=0))
        if mine:
            q, do = cqo[turn, span, :HD], cqo[turn, span, HD:].astype(F32)
            ds1 = qp_ds[half_at]
            dq = do + matmul_last(qp_dz[half_at], first) + matmul(ds1, k)
            g1 = m * slope
            dk = matmul_first(ds1, q) - matmul_last(spread(e) * g1, d1b) + dr + matmul_last(dz1b, first)
            de = row_sum(jnp.transpose(qp_kept[half_at])) - row_sum(p1 * g1) - row_sum(p2 * g2)
            dproj_ref[span, :HD] = dq.astype(BF16)
            dproj_ref[span, HD : 2 * HD] = dk.astype(BF16)
            dproj_ref[span, 2 * HD :] = (-dr).astype(BF16)
            dlogit_ref[span, :] = de * e * (1.0 - e * (HD / BASE_RATE))

    def share_out(step, source):
        to = lax.rem(head + step, heads)
        return pltpu.make_async_remote_copy(
            src_ref=send_out.at[to],
            dst_ref=recv_out.at[source],
            send_sem=out_send.at[to],
            recv_sem=out_recv.at[source],
            device_id={"head": to},
            device_id_type=MESH,
        )

    def send_terms():
        rows_out = ttt_ref[...]
        for step in range(1, heads):
            to = lax.rem(head + step, heads)
            send_out[to] = matmul_last(rows_out, out_rows(to)).astype(BF16)
            if step > 1:
                share_out(step - 1, head).start()
        recv_out[head] = matmul_last(rows_out, out_rows(head)).astype(BF16)
        share_out(heads - 1, head).start()

    def state_turn(turn, carry):
        @pl.when(turn + 2 < count)
        def _():
            take_chunk(turn + 2)

        rate_row = ckt[turn, rows:, :HD].astype(F32) + ckt[turn, rows:, HD:].astype(F32)
        spread_rates = jnp.transpose(jnp.broadcast_to(rate_row[:1, :], (HD, rows)))
        state_block(turn, 0, spread_rates[:MB])
        state_block(turn, 1, spread_rates[MB:])
        return carry

    def early_turn(turn, carry):
        state_turn(turn, 0)

        @pl.when(turn == 0)
        def _():
            ring_partner(cot, cot_recv)
            cot_step(ring_base, 2)
            wo_sides()

        @pl.when(turn == 1)
        def _():
            cot_step(other_base, 1)
            cot_step(ring_base, 3)
            wo_far()

        @pl.when(turn == 2)
        def _():
            cot_step(other_base, 2)
            cot_step(ring_base, 4)

        return carry

    def qo_copy(source, to):
        return pltpu.make_async_remote_copy(
            src_ref=cqo.at[source],
            dst_ref=cqo.at[source],
            send_sem=qo_send.at[to],
            recv_sem=qo_recv.at[source],
            device_id={"seq": to},
            device_id_type=MESH,
        )

    def late_turn(turn, carry):
        state_turn(turn, 0)

        @pl.when(turn == jnp.maximum(place, 3))
        def _():
            for half_at in range(2):
                parts = query_forward(place, half_at)
                ttt_ref[span_of(half_at), :] = (parts[0].astype(F32) + parts[-2]).astype(BF16)
            send_terms()

        @pl.when(turn == 3)
        def _():
            cot_step(other_base, 3)

        @pl.when(turn == 4)
        def _():
            cot_step(other_base, 4)
            d_ttt = jnp.zeros((rows, HD), F32)
            for piece in range(heads):
                d_ttt = d_ttt + jnp.dot(cot[piece], out_rows(piece), preferred_element_type=F32)
            cqo[place, :, HD:] = d_ttt.astype(BF16)

            def send_qo(to, carry):
                qo_copy(place, to).start()
                return carry

            lax.fori_loop(0, place, send_qo, 0)

        return carry

    take_chunk(0)
    take_chunk(1)
    lax.fori_loop(0, 3, early_turn, 0)
    for column in range(groups):
        wo_column_arrived(sib, column)
    lax.fori_loop(3, count, late_turn, 0)

    dw1_ref[...] = jnp.zeros_like(dw1_ref)
    dw2_ref[...] = jnp.zeros_like(dw2_ref)

    def take_qo(source):
        @pl.when(source > place)
        def _():
            qo_copy(source, place).wait_recv()

    take_qo(count - 1)
    query_part(count - 1, 1)

    def back_turn(step, carry):
        turn = count - 1 - step
        take_qo(turn - 1)
        chain_block(turn, 1, False)
        query_part(turn, 0)
        chain_block(turn, 0, False)
        query_part(turn - 1, 1)
        return carry

    lax.fori_loop(0, count - 1 - place, back_turn, 0)
    chain_block(place, 1, True)
    query_part(place, 0)
    chain_block(place, 0, True)

    def pair_copy(spot):
        return pltpu.make_async_remote_copy(
            src_ref=pair_send.at[spot],
            dst_ref=pair_recv.at[spot],
            send_sem=pair_sends.at[spot],
            recv_sem=pair_recvs.at[spot],
            device_id=partner,
            device_id_type=MESH,
        )

    def share_tok(spot, source):
        return pltpu.make_async_remote_copy(
            src_ref=send_tok.at[spot],
            dst_ref=recv_tok.at[source],
            send_sem=tok_send.at[spot],
            recv_sem=tok_recv.at[source],
            device_id={"head": ring_base + spot},
            device_id_type=MESH,
        )

    d_proj = dproj_ref[...]
    d_logit = jnp.concatenate([dlogit_ref[...], dlogit_ref[...]], axis=1)

    def token_term(to):
        return matmul_last(d_proj, depth_rows(wq, to)) + d_logit * rate_weights(to)

    spots = [lax.rem(ring_at + step, ring) for step in (4, 3, 5, 2, 6, 1, 7, 0)]
    for at, spot in enumerate(spots):
        pair_send[spot] = token_term(other_base + spot).astype(BF16)
        if at > 0:
            pair_copy(spots[at - 1]).start()
    last_pair = spots[-1]

    def dw_copy(step, source):
        to = lax.rem(group + step, groups)
        return pltpu.make_async_remote_copy(
            src_ref=dw_send.at[to],
            dst_ref=dw_recv.at[source],
            send_sem=dw_sems.at[step],
            recv_sem=dw_recvs.at[source],
            device_id={"dp": to},
            device_id_type=MESH,
        )

    def share_copy(to):
        return pltpu.make_async_remote_copy(
            src_ref=dw_sum.at[to],
            dst_ref=share,
            send_sem=share_send.at[to],
            recv_sem=share_recv,
            device_id={"seq": to},
            device_id_type=MESH,
        )

    @pl.when(place == 0)
    def _():
        joined = jnp.transpose(jnp.concatenate([dw1_ref[...], dw2_ref[...]], axis=0))
        parts = joined.reshape(count, groups, -1, 2 * HD)
        for part in range(groups):
            dw_send[part] = parts[:, part]
        for step in range(1, groups):
            dw_copy(step, group).start()

    for at, spot in enumerate(spots):
        term = token_term(ring_base + spot)
        if at == 0:
            pair_copy(last_pair).start()
        if at > 0:
            share_tok(spots[at - 1], ring_at).start()
        pair_copy(spot).wait_recv()
        term = (term + pair_recv[spot].astype(F32)).astype(BF16)
        if at < ring - 1:
            send_tok[spot] = term
        else:
            recv_tok[ring_at] = term

    @pl.when(place == 0)
    def _():
        total = dw_send[group]
        for step in range(1, groups):
            source = lax.rem(group + step, groups)
            dw_copy(step, source).wait_recv()
            total = total + dw_recv[source]
        dw_sum[...] = total
        share[...] = total[0]
        for to in range(1, count):
            share_copy(to).start()

    def sum_terms(copy, received):
        def add(step, total):
            source = lax.rem(head + step, heads)

            @pl.when(step > 0)
            def _():
                copy(0, source).wait_recv()

            return total + received[source].astype(F32)

        return lax.fori_loop(0, heads, add, jnp.zeros((rows, 2 * HD), F32)).astype(BF16)

    out_ref[...] = sum_terms(share_out, recv_out)
    total = recv_tok[ring_at].astype(F32)
    for step in (1, 7, 2, 6, 3, 5, 4):
        source = lax.rem(ring_at + step, ring)
        share_tok(ring_at, source).wait_recv()
        total = total + recv_tok[source].astype(F32)
    dtok_ref[...] = total.astype(BF16)

    @pl.when(place > 0)
    def _():
        share_copy(0).wait_recv()

    share1_ref[...] = share[:, :HD]
    share2_ref[...] = share[:, HD:]

    @pl.when(place == 0)
    def _():
        for step in range(1, groups):
            dw_copy(step, group).wait_send()
        for to in range(1, count):
            share_copy(to).wait_send()

    for which in range(4):
        chunk_copy(place, sib, count + which).wait_send()

    def sent_chunk(source, carry):
        @pl.when(same_side(source))
        def _():
            chunk_copy(source, sib, source).wait_send()

        return carry

    lax.fori_loop(0, count, sent_chunk, 0)

    def sent_qo(to, carry):
        qo_copy(place, to).wait_send()
        return carry

    lax.fori_loop(0, place, sent_qo, 0)

    def sent_terms(step, carry):
        share_out(step, head).wait_send()
        return carry

    lax.fori_loop(1, heads, sent_terms, 0)
    for spot in spots:
        pair_copy(spot).wait_send()
    for spot in spots[:-1]:
        share_tok(spot, ring_at).wait_send()
    views = [feat.at[0], wq.at[0], wq.at[0, :half], wo.at[0], wo.at[0, :half]]
    views += [wo.at[pl.ds(0, layers)], wo.at[pl.ds(0, layers // 2)]]
    view_of = {tuple(view.shape): view for view in views}
    for index, shape in enumerate(started):
        pltpu.make_async_remote_copy(
            src_ref=view_of[shape],
            dst_ref=view_of[shape],
            send_sem=near_send.at[index],
            recv_sem=feat_recv.at[0],
            device_id={"seq": place},
            device_id_type=MESH,
        ).wait_send()


def layer(tokens, w_qkv, w_lr, w_out, w_first, w_second, d_out):
    rows, width = tokens.shape
    peers, heads, groups = (lax.axis_size(name) for name in ("seq", "head", "dp"))
    inner = w_first.shape[1]
    share = inner // (peers * groups)
    blocks = peers * groups
    steps = peers * (rows // MB)
    vmem = pl.BlockSpec(memory_space=pltpu.VMEM)
    dma = pltpu.SemaphoreType.DMA
    return pl.pallas_call(
        layer_kernel,
        out_shape=(
            jax.ShapeDtypeStruct((rows, width), BF16),
            jax.ShapeDtypeStruct((rows, width), BF16),
            jax.ShapeDtypeStruct((share, HD), F32),
            jax.ShapeDtypeStruct((share, HD), F32),
        ),
        in_specs=[vmem] * 7,
        out_specs=(vmem,) * 4,
        scratch_shapes=[
            pltpu.VMEM((heads, rows, width), BF16),
            pltpu.VMEM((heads, rows, width), BF16),
            pltpu.VMEM((blocks, rows, 3 * HD), BF16),
            pltpu.VMEM((blocks, rows, HD), BF16),
            pltpu.VMEM((rows, HD), BF16),
            pltpu.VMEM((rows, 3 * HD), BF16),
            pltpu.VMEM((rows, HD), F32),
            pltpu.VMEM((HD, inner), F32),
            pltpu.VMEM((HD, inner), F32),
            pltpu.VMEM((heads, rows, width), BF16),
            pltpu.VMEM((heads, rows, width), BF16),
            pltpu.VMEM((heads // 2, rows, width), BF16),
            pltpu.VMEM((heads // 2, rows, width), BF16),
            pltpu.VMEM((heads // 2, rows, width), BF16),
            pltpu.VMEM((heads // 2, rows, width), BF16),
            pltpu.VMEM((groups, peers, share, 2 * HD), F32),
            pltpu.VMEM((groups, peers, share, 2 * HD), F32),
            pltpu.VMEM((peers, share, 2 * HD), F32),
            pltpu.VMEM((share, 2 * HD), F32),
            pltpu.VMEM((peers, rows + 16, 2 * HD), BF16),
            pltpu.VMEM((peers, rows, 2 * HD), BF16),
            pltpu.VMEM((HD, inner), F32),
            pltpu.VMEM((inner, HD), F32),
            pltpu.VMEM((steps, HD, inner), BF16),
            pltpu.VMEM((steps, inner, HD), BF16),
            pltpu.VMEM((steps, MB, inner), F32),
            pltpu.VMEM((steps, MB, inner), F32),
            pltpu.VMEM((steps, MB, inner), F32),
            pltpu.VMEM((steps, MB, inner), BF16),
            pltpu.VMEM((steps, 7, MB, HD), F32),
            pltpu.VMEM((2, MB, inner), BF16),
            pltpu.VMEM((2, MB, HD), BF16),
            pltpu.VMEM((2, 2, MB, inner), F32),
            pltpu.VMEM((2, MB, HD), F32),
            pltpu.VMEM((2, MB, inner), BF16),
            pltpu.VMEM((2, MB, MB), BF16),
            pltpu.VMEM((2, MB, MB), F32),
            dma((96,)),
            dma((heads,)),
            dma((heads,)),
            dma((blocks,)),
            dma((blocks,)),
            dma((blocks + 2 * groups,)),
            dma((blocks + 2 * groups,)),
            dma((peers + 4,)),
            dma((peers,)),
            dma((peers,)),
            dma((peers,)),
            dma((heads,)),
            dma((heads,)),
            dma((heads // 2,)),
            dma((heads // 2,)),
            dma((heads // 2,)),
            dma((heads // 2,)),
            dma((groups,)),
            dma((groups,)),
            dma((peers,)),
            dma(()),
        ],
        compiler_params=pltpu.CompilerParams(collective_id=0, has_side_effects=True),
        name="layer",
    )(tokens, w_qkv, w_lr, w_out, w_first, w_second, d_out)


def body(tokens, w_qkv, w_lr, w_out, w1_init, w2_init, d_out):
    out, d_tokens, share_first, share_second = layer(
        tokens[0],
        w_qkv,
        w_lr.astype(F32).reshape(-1, HD),
        w_out,
        w1_init[0],
        w2_init[0],
        d_out[0],
    )
    return (out[None], d_tokens[None], share_first.transpose(1, 0)[None], share_second[None])


def solution(mesh):
    placed = (
        P("dp", "seq", "head"),
        P(("seq", "dp"), None, "head"),
        P(None, "head"),
        P(("seq", "dp"), "head"),
        P("head", None, None),
        P("head", None, None),
        P("dp", "seq", "head"),
    )
    return jax.shard_map(
        body,
        mesh=mesh,
        in_specs=placed,
        out_specs=(
            P("dp", "seq", "head"),
            P("dp", "seq", "head"),
            P("head", None, ("seq", "dp")),
            P("head", ("seq", "dp"), None),
        ),
        check_vma=False,
    )
```

profile of v0, /device:TPU:1, one launch (start us, length us, event | category | flops | bytes accessed | tf_op | source)
XLA Modules:
  0.0 145.4 jit_solution(12462255510497873465)
XLA Ops:
  0.6 1.3 reshape.15
  2.0 1.6 %copy.11.wqkv_ref = bf16[128,3,128]{2,1,0:T(4,128)(2,1)} copy(bf16[128,3,128]{2,0,1:T(8,128)(2,1)} %param.8) | data formatting | bytes 196608 | tf_op args[1]
  3.6 138.3 %layer.1 = (bf16[128,256]{1,0:T(8,128)(2,1)}, bf16[128,256]{1,0:T(8,128)(2,1)}, f32[16,128]{1,0:T(8,128)}, f32[16,128]{1,0:T(8,128)}) custom-call(bf16[128,256]{1,0:T(8,128)(2,1)} %bitcast.13, bf16[128,3,128]{2,1,0:T(4,128)(2,1)} %copy.11.wqkv_ref, f32[32,128]{1,0:T(8,128)} %bitcast.15, bf16[128,128]{1,0:T(8,128)(2,1)} %wout_ref.1, f32[128,512]{1,0:T(8,128)} %bitcast.11, ...), custom_call_target="tpu_custom_call" | custom-call | tf_op jit(solution)/shard_map/layer/pallas_call | solution.py:768
  141.9 0.0 copy-start
  141.9 1.5 %copy.16 = bf16[1,128,256]{2,1,0:T(8,128)(2,1)} copy(bf16[1,128,256]{2,1,0:T(8,128)(2,1)} %bitcast.17) | data formatting | bytes 131072
  143.4 0.0 copy-done
  143.4 0.0 copy-start.2
  143.4 0.6 copy.17
  144.0 0.1 copy-done.2
  144.1 0.0 copy-start.1
  144.1 0.6 copy.18
  144.7 0.1 copy-done.1
  144.8 0.6 copy.19
Async XLA Ops:
  141.9 1.5 %copy-start = (bf16[128,256]{1,0:T(8,128)(2,1)S(1)}, bf16[128,256]{1,0:T(8,128)(2,1)}, u32[]{:S(2)}) copy-start(bf16[128,256]{1,0:T(8,128)(2,1)} %get-tuple-element.9) | copy-start | bytes 196612
  143.4 0.7 copy-start.2
  144.1 0.7 copy-start.1
where the time goes:
time: 148 us; the launch traced here: 145 us
  Pallas kernels  138 us (93%)
  local copies, waits for them, and re-layouts  5.13 us (3%)
    pallas_call x1, Pallas kernels, layer(): pl.pallas_call(layer_kernel, out_shape=(jax.ShapeDtypeStruct((rows, width...  138 us
    unnamed x11, local copies, waits for them, and re-layouts  5.13 us

commit v1 on v0

--- a/solution.py
+++ b/solution.py
@@ -131,7 +131,6 @@
     def ring_start(buffer, arrivals, src):
         ring_push(buffer, arrivals, head, ring_up, src)
         ring_push(buffer, arrivals, head, ring_down, src)
-        ring_push(buffer, arrivals, head, partner, src)
 
     def ring_partner(buffer, arrivals):
         block = other_base + ring_at
@@ -250,12 +249,11 @@
     wq_push(own, deep_up)
     wq_push(own, deep_down)
     wq_spread(place)
-    push(wout_ref, wo.at[own_wo], wo_recv.at[own_wo], deep_up)
-    push(wout_ref, wo.at[own_wo], wo_recv.at[own_wo], deep_down)
     feat[head] = tok_ref[...]
     cot[head] = dout_ref[...]
     wo[own_wo] = wout_ref[...]
     feat_step(ring_base, 1)
+    ring_push(feat, feat_recv, head, partner, tok_ref)
     wq_sides(place)
     ring_partner(feat, feat_recv)
     feat_step(ring_base, 2)
@@ -264,12 +262,11 @@
     wq_relay(deep[3] * groups + group, deep[1] * groups + group, deep_up, deep_down)
     wq_spread(deep[3])
     wq_spread(deep[1])
+    push(wout_ref, wo.at[own_wo], wo_recv.at[own_wo], deep_up)
+    push(wout_ref, wo.at[own_wo], wo_recv.at[own_wo], deep_down)
     wq_far(place)
     feat_step(other_base, 1)
     feat_step(ring_base, 3)
-    for row in (deep[3], deep[1]):
-        arrived(wo.at[wo_block(row, group)], wo_recv.at[wo_block(row, group)])
-    wo_relay(wo_block(deep[3], group), wo_block(deep[1], group), deep_up, deep_down)
     feat_step(other_base, 2)
     wq_halves_arrived(deep[2] * groups + group)
     wq_spread(deep[2])
@@ -278,18 +275,21 @@
     feat_step(ring_base, 4)
     feat_step(other_base, 3)
     ring_start(cot, cot_recv, dout_ref)
-    far = wo_block(deep[2], group)
-    arrived(wo.at[far, :half], wo_recv.at[far])
-    arrived(wo.at[far, half:], wo_recv_low.at[far])
+    for row in (deep[3], deep[1]):
+        arrived(wo.at[wo_block(row, group)], wo_recv.at[wo_block(row, group)])
+    wo_relay(wo_block(deep[3], group), wo_block(deep[1], group), deep_up, deep_down)
     wq_sides(deep[2])
-    wo_column_push(group, wide_up)
-    wo_column_push(group, wide_down)
-    wo_column_push(group, sibling)
     feat_step(other_base, 4)
     wq_far(deep[3])
     wq_far(deep[1])
     cot_step(ring_base, 1)
     wq_far(deep[2])
+    far = wo_block(deep[2], group)
+    arrived(wo.at[far, :half], wo_recv.at[far])
+    arrived(wo.at[far, half:], wo_recv_low.at[far])
+    wo_column_push(group, wide_up)
+    wo_column_push(group, wide_down)
+    wo_column_push(group, sibling)
     for row in sib_deep:
         for column in (0, 1, 3, 2):
             wq_arrived(row * groups + wide[column])
@@ -339,10 +339,18 @@
 
     s1[...] = w1_ref[...]
     s2[...] = w2_ref[...]
-    chunk_copy(place, deep[1], count).start()
-    chunk_copy(place, deep[3], count + 1).start()
-    chunk_copy(place, sib, count + 2).start()
-    chunk_copy(place, deep[2], count + 3).start()
+
+    def send_chunk():
+        chunk_copy(place, deep[1], count).start()
+        chunk_copy(place, deep[3], count + 1).start()
+        chunk_copy(place, sib, count + 2).start()
+        chunk_copy(place, deep[2], count + 3).start()
+
+    @pl.when(place < 4)
+    def _():
+        send_chunk()
+
+    ring_push(cot, cot_recv, head, partner, dout_ref)
 
     def same_side(source):
         return jnp.logical_and(source != place, lax.rem(source + place, 2) == 0)
@@ -500,6 +508,10 @@
         return carry
 
     def early_turn(turn, carry):
+        @pl.when(jnp.logical_and(place >= 4, turn == jnp.maximum(place - 5, 0)))
+        def _():
+            send_chunk()
+
         state_turn(turn, 0)
 
         @pl.when(turn == 0)
@@ -534,7 +546,7 @@
     def late_turn(turn, carry):
         state_turn(turn, 0)
 
-        @pl.when(turn == jnp.maximum(place, 3))
+        @pl.when(turn == jnp.maximum(place, 5))
         def _():
             for half_at in range(2):
                 parts = query_forward(place, half_at)

time: 148 us -> 138 us (0.932)
  Pallas kernels: 138 us -> 129 us
    pallas_call x1, Pallas kernels: 138 us -> 129 us  [layer(): pl.pallas_call(layer_kernel, out_shape=(jax.ShapeDtypeStruct((rows, width...]
where the time goes in v1:
time: 138 us; the launch traced here: 137 us
  Pallas kernels  129 us (93%)
  local copies, waits for them, and re-layouts  5.13 us (4%)
    pallas_call x1, Pallas kernels, layer(): pl.pallas_call(layer_kernel, out_shape=(jax.ShapeDtypeStruct((rows, width...  129 us
    unnamed x11, local copies, waits for them, and re-layouts  5.13 us

profile of v1, /device:TPU:1, one launch (start us, length us, event | category | flops | bytes accessed | tf_op | source)
XLA Modules:
  0.0 136.6 jit_solution(7104644668182134898)
XLA Ops:
  0.6 1.3 reshape.15
  2.0 1.6 %copy.11.wqkv_ref = bf16[128,3,128]{2,1,0:T(4,128)(2,1)} copy(bf16[128,3,128]{2,0,1:T(8,128)(2,1)} %param.8) | data formatting | bytes 196608 | tf_op args[1]
  3.6 129.5 %layer.1 = (bf16[128,256]{1,0:T(8,128)(2,1)}, bf16[128,256]{1,0:T(8,128)(2,1)}, f32[16,128]{1,0:T(8,128)}, f32[16,128]{1,0:T(8,128)}) custom-call(bf16[128,256]{1,0:T(8,128)(2,1)} %bitcast.13, bf16[128,3,128]{2,1,0:T(4,128)(2,1)} %copy.11.wqkv_ref, f32[32,128]{1,0:T(8,128)} %bitcast.15, bf16[128,128]{1,0:T(8,128)(2,1)} %wout_ref.1, f32[128,512]{1,0:T(8,128)} %bitcast.11, ...), custom_call_target="tpu_custom_call" | custom-call | tf_op jit(solution)/shard_map/layer/pallas_call | solution.py:780
  133.1 0.0 copy-start
  133.1 1.5 %copy.16 = bf16[1,128,256]{2,1,0:T(8,128)(2,1)} copy(bf16[1,128,256]{2,1,0:T(8,128)(2,1)} %bitcast.17) | data formatting | bytes 131072
  134.6 0.0 copy-done
  134.6 0.0 copy-start.2
  134.6 0.6 copy.17
  135.2 0.1 copy-done.2
  135.3 0.0 copy-start.1
  135.3 0.6 copy.18
  135.9 0.1 copy-done.1
  136.0 0.6 copy.19
Async XLA Ops:
  133.1 1.5 %copy-start = (bf16[128,256]{1,0:T(8,128)(2,1)S(1)}, bf16[128,256]{1,0:T(8,128)(2,1)}, u32[]{:S(2)}) copy-start(bf16[128,256]{1,0:T(8,128)(2,1)} %get-tuple-element.9) | copy-start | bytes 196612
  134.6 0.7 copy-start.2
  135.3 0.7 copy-start.1
